TPU v7x, 32 devices: a whole 2x2x4 slice. The times are simulated.
32 devices in a mesh: groups: 2 (over y), dp: 2 (over core), tensor: 8 (over z, x).
Axes of the slice: x: 2, y: 2, z: 4, core: 2. Of those that a mesh axis runs over, the one named last changes fastest.
Arguments:
- tokens: bfloat16 [512, 8192], P(('groups', 'dp', 'tensor')), parts along dimension 0, may hold values from -134 to 134
- ln_gain: float32 [8192], replicated, may hold values from 0.25 to 1.75
- gate_weight: bfloat16 [8192, 16384], P('dp', 'tensor'), may hold values from -0.09375 to 0.09375
- up_weight: bfloat16 [8192, 16384], P('dp', 'tensor'), may hold values from -0.09375 to 0.09375
- down_weight: bfloat16 [16384, 8192], P('tensor', 'dp'), may hold values from -0.0625 to 0.0625
- gate_mask: int32 [64, 128], replicated, may hold values from 0 to 1, as said below
- up_mask: int32 [64, 128], replicated, may hold values from 0 to 1, as said below
- down_mask: int32 [128, 64], replicated, may hold values from 0 to 1, as said below
Outputs:
- mlp_out: bfloat16 [512, 8192], P(('groups', 'dp', 'tensor')), parts along dimension 0
There are 2 independent parts, one for each index of `groups`. A program takes and returns all parts, laid end to end along the dimension named above; an argument that names none is the same for every part. Nothing has to cross between parts.
Inputs may be any that keep to these rules, and one draw needn't show every extreme that they name: `gate_mask`: in every block column, each of the 2 owners' runs of 32 consecutive block rows holds at least one and at most 24 ones; in some column every owner's run holds exactly 24. `up_mask`: as gate_mask. `down_mask`: in every block row, each of the 2 owners' runs of 32 consecutive block columns holds at least one and at most 24 ones; in some row every owner's run holds exactly 24.
All inputs are finite; a program needn't handle non-finite values.
Results may differ from a plain program's by a relative error of at most 0.0065.
Values may be sent and summed in bfloat16 or wider, within the bound.
A program may use at most 448 MiB of HBM per device.

v0:
```python
import functools

import jax
import jax.numpy as jnp
from jax import lax
from jax.experimental import pallas as pl
from jax.experimental.pallas import tpu as pltpu
from jax.sharding import PartitionSpec as P

BLK = 128
ROWS = 16
NC = 256
GRP = 512
DCH = 1024
EPSILON = 1e-05
F32 = jnp.float32
BF16 = jnp.bfloat16


def layer_norm(tokens, ln_gain):
    values = tokens.astype(F32)
    average = jnp.mean(values, axis=1, keepdims=True)
    centered = values - average
    variance = jnp.mean(centered * centered, axis=1, keepdims=True)
    return (centered * lax.rsqrt(variance + EPSILON) * ln_gain).astype(BF16)


def expand(mask, dtype):
    return jnp.repeat(jnp.repeat(mask.astype(dtype), BLK, axis=0), BLK, axis=1)


def general(tokens, ln_gain, gate_weight, up_weight, down_weight, gate_mask, up_mask, down_mask):
    t = lax.axis_index("tensor")
    d = lax.axis_index("dp")
    kl, fl = gate_weight.shape
    kb, fb = kl // BLK, fl // BLK
    normed = layer_norm(tokens, ln_gain)
    rows = lax.all_gather(normed, ("dp", "tensor"), axis=0, tiled=True)
    mine = lax.dynamic_slice_in_dim(rows, d * kl, kl, 1)

    def cut(mask, r0, c0, nr, nc):
        return expand(lax.dynamic_slice(mask, (r0, c0), (nr, nc)), BF16)

    gw = gate_weight * cut(gate_mask, d * kb, t * fb, kb, fb)
    uw = up_weight * cut(up_mask, d * kb, t * fb, kb, fb)
    dw = down_weight * cut(down_mask, t * fb, d * kb, fb, kb)
    gate = lax.psum(jnp.dot(mine, gw, preferred_element_type=F32), "dp")
    up = lax.psum(jnp.dot(mine, uw, preferred_element_type=F32), "dp")
    hidden = (jax.nn.silu(gate) * up).astype(BF16)
    part = jnp.dot(hidden, dw, preferred_element_type=F32)
    full = lax.all_gather(part, "dp", axis=1, tiled=True)
    half = full.shape[0] // lax.axis_size("dp")
    full = lax.dynamic_slice_in_dim(full, d * half, half, 0)
    return lax.psum_scatter(full, "tensor", scatter_dimension=0, tiled=True).astype(BF16)


def fused_kernel(
    Z,
    gm, um, dm, tok, gain, gw_hbm, uw_hbm, dw_hbm,
    out,
    gw, uw, dw, nrm, xbuf, exs, exr, own, hid, sb, acc, rx, zs, zr, fin, finrx,
    w_sem, in_s, in_r, agz_s, agz_r, agx_s, agx_r, ex_s, ex_r, hd_s, hd_r,
    rx_s, rx_r, rz_s, rz_r, fn_s, fn_r,
):
    kl, fl = gw.shape
    kb, fb = kl // BLK, fl // BLK
    half = fl // 2
    line = Z * ROWS
    groups = half // GRP
    chunks = kl // DCH
    d = lax.axis_index("dp")
    t = lax.axis_index("tensor")
    z = t // 2
    x = t % 2
    peer = {"dp": 1 - d}
    xnbr = {"tensor": z * 2 + (1 - x)}

    def zdev(i):
        return {"tensor": lax.rem(z + i, Z) * 2 + x}

    def zsrc(i):
        return lax.rem(z + Z - i, Z)

    def slot(j):
        return pl.ds(pl.multiple_of(j * ROWS, ROWS), ROWS)

    def remote(src, dst, ss, rs, dev):
        return pltpu.make_async_remote_copy(
            src_ref=src, dst_ref=dst, send_sem=ss, recv_sem=rs,
            device_id=dev, device_id_type=pl.DeviceIdType.MESH,
        )

    def wcopy(k):
        which, part = k // 4, k % 4
        src, dst = ((gw_hbm, gw), (uw_hbm, uw), (dw_hbm, dw))[which]
        n = src.shape[0] // 4
        return pltpu.make_async_copy(
            src.at[pl.ds(part * n, n), :], dst.at[pl.ds(part * n, n), :], w_sem.at[k]
        )

    for k in range(12):
        wcopy(k).start()

    barrier = pltpu.get_barrier_semaphore()
    for dev in [peer, xnbr] + [zdev(i) for i in range(1, Z)]:
        pl.semaphore_signal(barrier, inc=1, device_id=dev, device_id_type=pl.DeviceIdType.MESH)

    values = tok[...].astype(F32)
    average = jnp.mean(values, axis=1, keepdims=True)
    centered = values - average
    variance = jnp.mean(centered * centered, axis=1, keepdims=True)
    nrm[...] = (centered * lax.rsqrt(variance + EPSILON) * gain[...]).astype(BF16)

    pl.semaphore_wait(barrier, Z + 1)

    def cols(o):
        return pl.ds(pl.multiple_of(o * kl, kl), kl)

    first = remote(nrm.at[:, cols(1 - d)], xbuf.at[d, slot(z), :], in_s, in_r, peer)
    first.start()
    xbuf[d, slot(z), :] = nrm[:, cols(d)]
    remote(nrm.at[:, cols(d)], xbuf.at[1 - d, slot(z), :], in_s, in_r, peer).wait_recv()

    def agz(h, i):
        return remote(xbuf.at[h, slot(z), :], xbuf.at[h, slot(z), :],
                      agz_s.at[h, i - 1], agz_r.at[h, i - 1], zdev(i))

    def agz_in(h, i):
        blk = xbuf.at[h, slot(zsrc(i)), :]
        return remote(blk, blk, agz_s.at[h, i - 1], agz_r.at[h, i - 1], zdev(i))

    def agx(h, i):
        return remote(xbuf.at[h, slot(zsrc(i)), :], xbuf.at[h, slot(Z + zsrc(i)), :],
                      agx_s.at[h, i], agx_r.at[h, i], xnbr)

    def ag_start(h):
        agx(h, 0).start()
        for i in range(1, Z):
            agz(h, i).start()

    def ag_forward(h, i):
        agz_in(h, i).wait_recv()
        agx(h, i).start()

    def ag_finish(h):
        for i in range(Z):
            agx(h, i).wait_recv()

    def prune(k):
        wcopy(k).wait()
        which, part = k // 4, k % 4
        w = (gw, uw, dw)[which]
        m = (gm, um, dm)[which]
        nr, nc = w.shape[0] // BLK, w.shape[1] // BLK
        if which == 2:
            r0, c0 = t * nr, d * nc
        else:
            r0, c0 = d * nr, t * nc
        n = nr // 4

        def body(b, carry):
            rb = part * n + b
            rows = pl.ds(pl.multiple_of(rb * BLK, BLK), BLK)
            for cb in range(nc):
                keep = jnp.full((16, BLK), m[r0 + rb, c0 + cb].astype(F32), F32).astype(BF16)
                tile = w[rows, cb * BLK:(cb + 1) * BLK].reshape(BLK // 16, 16, BLK)
                w[rows, cb * BLK:(cb + 1) * BLK] = (tile * keep[None]).reshape(BLK, BLK)
            return carry

        lax.fori_loop(0, n, body, 0)

    def group(h, q, mine):
        base = (d if mine else 1 - d) * half + q * GRP

        def body(c, carry):
            cs = pl.ds(pl.multiple_of(base + c * NC, NC), NC)
            g = jnp.dot(xbuf[h], gw[:, cs], preferred_element_type=F32)
            u = jnp.dot(xbuf[h], uw[:, cs], preferred_element_type=F32)
            os = pl.ds(pl.multiple_of(c * NC, NC), NC)
            dst = own if mine else exs
            dst[q, 0, :, os] = g
            dst[q, 1, :, os] = u
            return carry

        lax.fori_loop(0, GRP // NC, body, 0)
        if not mine:
            ex(h, q).start()

    def ex(h, q):
        return remote(exs.at[q], exr.at[q], ex_s.at[h, q], ex_r.at[h, q], peer)

    def hcols(o, q):
        return pl.ds(pl.multiple_of(o * half + q * GRP, GRP), GRP)

    def hd(h, q, o):
        blk = hid.at[:, hcols(o, q)]
        return remote(blk, blk, hd_s.at[h, q], hd_r.at[h, q], peer)

    def hidden(h):
        for q in range(groups):
            ex(h, q).wait()
            g = own[q, 0] + exr[q, 0]
            u = own[q, 1] + exr[q, 1]
            hid[:, hcols(d, q)] = (g / (1.0 + jnp.exp(-g)) * u).astype(BF16)
            hd(h, q, d).start()
        for q in range(groups):
            hd(h, q, 1 - d).wait_recv()

    def chunk(c):
        return pl.ds(c * DCH, DCH)

    def rsx(h, c):
        return remote(sb.at[:, chunk(c)], rx.at[h, :, chunk(c)], rx_s.at[h, c], rx_r.at[h, c], xnbr)

    def down(h):
        for c in range(chunks):
            def body(j, carry):
                cs = pl.ds(pl.multiple_of(c * DCH + j * NC, NC), NC)
                p = jnp.dot(hid[...], dw[:, cs], preferred_element_type=F32)
                acc[:, cs] = p[:line]
                sb[:, cs] = p[line:].astype(BF16)
                return carry

            lax.fori_loop(0, DCH // NC, body, 0)
            rsx(h, c).start()
        for q in range(groups):
            hd(h, q, d).wait_send()

    def rsz(h, c, i):
        return remote(zs.at[slot(lax.rem(z + i, Z)), chunk(c)], zr.at[h, i - 1, :, chunk(c)],
                      rz_s.at[h, c, i - 1], rz_r.at[h, c, i - 1], zdev(i))

    def rs_step(h, c):
        rsx(h, c).wait()
        total = acc[:, chunk(c)] + rx[h, :, chunk(c)].astype(F32)
        acc[:, chunk(c)] = total
        zs[:, chunk(c)] = total.astype(BF16)
        for i in range(1, Z):
            rsz(h, c, i).start()

    def rs_final(h):
        for c in range(chunks):
            for i in range(1, Z):
                rsz(h, c, i).wait()
            total = acc[slot(z), chunk(c)]
            for i in range(1, Z):
                total = total + zr[h, i - 1, :, chunk(c)].astype(F32)
            fin[h, :, chunk(c)] = total.astype(BF16)

    ag_start(0)
    order = list(range(12))
    per = 2
    for i in range(1, Z):
        for k in order[:per]:
            prune(k)
        order = order[per:]
        ag_forward(0, i)
    ag_start(1)
    for k in order:
        prune(k)
    ag_finish(0)
    plan = [(q, False) for q in range(groups)] + [(q, True) for q in range(groups)]
    for n, (q, mine) in enumerate(plan):
        group(0, q, mine)
        if n + 1 < Z:
            ag_forward(1, n + 1)
    hidden(0)
    down(0)
    ag_finish(1)
    for n, (q, mine) in enumerate(plan):
        group(1, q, mine)
        rs_step(0, n)
    hidden(1)
    rs_final(0)
    down(1)
    for c in range(chunks):
        rs_step(1, c)
    rs_final(1)

    last = remote(fin.at[1 - d], finrx, fn_s, fn_r, peer)
    last.start()
    out[:, cols(d)] = fin[d]
    last.wait()
    out[:, cols(1 - d)] = finrx[...]
    first.wait_send()
    for h in range(2):
        for i in range(Z):
            agx(h, i).wait_send()
        for i in range(1, Z):
            agz(h, i).wait_send()


def fused(Z, tokens, ln_gain, gate_weight, up_weight, down_weight, gate_mask, up_mask, down_mask):
    kl, fl = gate_weight.shape
    dim = tokens.shape[1]
    half = fl // 2
    groups = half // GRP
    chunks = kl // DCH
    line = Z * ROWS
    m = 2 * line
    dma = pltpu.SemaphoreType.DMA
    vm = pl.BlockSpec(memory_space=pltpu.VMEM)
    sm = pl.BlockSpec(memory_space=pltpu.SMEM)
    hbm = pl.BlockSpec(memory_space=pl.ANY)
    flops = 2 * 2 * m * kl * fl * 3
    return pl.pallas_call(
        functools.partial(fused_kernel, Z),
        out_shape=jax.ShapeDtypeStruct((ROWS, dim), BF16),
        in_specs=[sm, sm, sm, vm, vm, hbm, hbm, hbm],
        out_specs=vm,
        scratch_shapes=[
            pltpu.VMEM((kl, fl), BF16),
            pltpu.VMEM((kl, fl), BF16),
            pltpu.VMEM((fl, kl), BF16),
            pltpu.VMEM((ROWS, dim), BF16),
            pltpu.VMEM((2, m, kl), BF16),
            pltpu.VMEM((groups, 2, m, GRP), F32),
            pltpu.VMEM((groups, 2, m, GRP), F32),
            pltpu.VMEM((groups, 2, m, GRP), F32),
            pltpu.VMEM((m, fl), BF16),
            pltpu.VMEM((line, kl), BF16),
            pltpu.VMEM((line, kl), F32),
            pltpu.VMEM((2, line, kl), BF16),
            pltpu.VMEM((line, kl), BF16),
            pltpu.VMEM((2, Z - 1, ROWS, kl), BF16),
            pltpu.VMEM((2, ROWS, kl), BF16),
            pltpu.VMEM((ROWS, kl), BF16),
            dma((12,)),
            dma, dma,
            dma((2, Z - 1)), dma((2, Z - 1)),
            dma((2, Z)), dma((2, Z)),
            dma((2, groups)), dma((2, groups)),
            dma((2, groups)), dma((2, groups)),
            dma((2, chunks)), dma((2, chunks)),
            dma((2, chunks, Z - 1)), dma((2, chunks, Z - 1)),
            dma, dma,
        ],
        compiler_params=pltpu.CompilerParams(
            collective_id=0, has_side_effects=True, vmem_limit_bytes=63 * 1024 * 1024
        ),
        cost_estimate=pl.CostEstimate(
            flops=flops, bytes_accessed=6 * kl * fl, transcendentals=0
        ),
    )(gate_mask, up_mask, down_mask, tokens, ln_gain.reshape(1, dim),
      gate_weight, up_weight, down_weight)


def solution(mesh):
    tensor = mesh.shape["tensor"]
    owners = mesh.shape["dp"]
    copies = mesh.shape["groups"]
    Z = tensor // 2

    def per_device(tokens, ln_gain, gate_weight, *rest):
        rows = tokens.shape[0]
        kl, fl = gate_weight.shape
        fits = (
            owners == 2 and tensor == 2 * Z and rows == ROWS and Z == 4
            and kl == 4 * DCH and fl == 4 * GRP
        )
        if fits:
            return fused(Z, tokens, ln_gain, gate_weight, *rest)
        return general(tokens, ln_gain, gate_weight, *rest)

    in_specs = (
        P(("groups", "dp", "tensor"), None),
        P(),
        P("dp", "tensor"),
        P("dp", "tensor"),
        P("tensor", "dp"),
        P(),
        P(),
        P(),
    )
    out_specs = P(("groups", "dp", "tensor"), None)
    return jax.shard_map(
        per_device, mesh=mesh, in_specs=in_specs, out_specs=out_specs, check_vma=False
    )
```

profile of v0, /device:TPU:0, one launch (start us, length us, event | category | flops | bytes accessed | tf_op | source)
XLA Modules:
  0.0 83.0 jit_solution(7327082640384657927)
XLA Ops:
  0.0 1.5 %copy.9.dm = s32[128,64]{1,0:T(8,128)} copy(s32[128,64]{0,1:T(8,128)} %param.15) | data formatting | bytes 65536 | tf_op args[7]
  1.5 79.8 %shard_map.82 = bf16[16,8192]{1,0:T(8,128)(2,1)} custom-call(s32[64,128]{1,0:T(8,128)} %gm.1, s32[64,128]{1,0:T(8,128)} %um.1, s32[128,64]{1,0:T(8,128)} %copy.9.dm, bf16[16,8192]{1,0:T(8,128)(2,1)} %tok.1, f32[1,8192]{1,0:T(1,128)} %bitcast.1, bf16[4096,2048]{1,0:T(8,128)(2,1)} %gw_hbm.1, bf16[4096,2048]{1,0:T(8,128)(2,1)} %uw_hbm.1, bf16[2048,4096]{1,0:T(8,128)(2,1)} %dw_hbm.1), custom_call_target="tpu_custom_call" | custom-call | flops 12884901888 | bytes 50331648 | tf_op jit(solution)/shard_map/pallas_call | solution.py:306
  81.3 1.7 %copy.11 = bf16[16,8192]{1,0:T(8,128)(2,1)} copy(bf16[16,8192]{1,0:T(8,128)(2,1)} %shard_map.82) | data formatting | bytes 524288
where the time goes:
time: 83.2 us; the launch traced here: 83 us
  Pallas kernels  79.8 us (96%)
  local copies, waits for them, and re-layouts  3.16 us (4%)
    pallas_call x1, Pallas kernels, fused(): pl.pallas_call(functools.partial(fused_kernel, Z), out_shape=jax.ShapeDty...  79.8 us
    unnamed x2, local copies, waits for them, and re-layouts  3.16 us

commit v1 on v0

--- a/solution.py
+++ b/solution.py
@@ -12,6 +12,8 @@
 NC = 256
 GRP = 512
 DCH = 1024
+AHEAD = 4
+SUB = 2
 EPSILON = 1e-05
 F32 = jnp.float32
 BF16 = jnp.bfloat16
@@ -98,7 +100,7 @@
             src.at[pl.ds(part * n, n), :], dst.at[pl.ds(part * n, n), :], w_sem.at[k]
         )
 
-    for k in range(12):
+    for k in range(AHEAD):
         wcopy(k).start()
 
     barrier = pltpu.get_barrier_semaphore()
@@ -121,33 +123,50 @@
     xbuf[d, slot(z), :] = nrm[:, cols(d)]
     remote(nrm.at[:, cols(d)], xbuf.at[1 - d, slot(z), :], in_s, in_r, peer).wait_recv()
 
-    def agz(h, i):
-        return remote(xbuf.at[h, slot(z), :], xbuf.at[h, slot(z), :],
-                      agz_s.at[h, i - 1], agz_r.at[h, i - 1], zdev(i))
-
-    def agz_in(h, i):
-        blk = xbuf.at[h, slot(zsrc(i)), :]
-        return remote(blk, blk, agz_s.at[h, i - 1], agz_r.at[h, i - 1], zdev(i))
-
-    def agx(h, i):
-        return remote(xbuf.at[h, slot(zsrc(i)), :], xbuf.at[h, slot(Z + zsrc(i)), :],
-                      agx_s.at[h, i], agx_r.at[h, i], xnbr)
+    def block(h, j, u):
+        return xbuf.at[h, slot(j), pl.ds(u * (kl // SUB), kl // SUB)]
+
+    def agz(h, j, side, s, u):
+        to = {"tensor": (z + 1 - 2 * side) * 2 + x}
+        return remote(block(h, j, u), block(h, j, u), agz_s.at[h, side, s * SUB + u],
+                      agz_r.at[h, j * SUB + u], to)
+
+    def agx(h, j, u):
+        return remote(block(h, j, u), block(h, Z + j, u), agx_s.at[h, j * SUB + u],
+                      agx_r.at[h, j * SUB + u], xnbr)
+
+    def relay(h, s, u, act):
+        pl.when((z >= s) & (z < Z - 1))(lambda: act(agz(h, z - s, 0, s, u)))
+        pl.when((z + s < Z) & (z > 0))(lambda: act(agz(h, z + s, 1, s, u)))
 
     def ag_start(h):
-        agx(h, 0).start()
-        for i in range(1, Z):
-            agz(h, i).start()
-
-    def ag_forward(h, i):
-        agz_in(h, i).wait_recv()
-        agx(h, i).start()
+        for u in range(SUB):
+            relay(h, 0, u, lambda c: c.start())
+            agx(h, z, u).start()
+
+    def ag_hop(h, s):
+        for u in range(SUB):
+            @pl.when(z >= s)
+            def _():
+                agz(h, z - s, 0, s, u).wait_recv()
+                pl.when(z < Z - 1)(lambda: agz(h, z - s, 0, s, u).start())
+                agx(h, z - s, u).start()
+
+            @pl.when(z + s < Z)
+            def _():
+                agz(h, z + s, 1, s, u).wait_recv()
+                pl.when(z > 0)(lambda: agz(h, z + s, 1, s, u).start())
+                agx(h, z + s, u).start()
 
     def ag_finish(h):
-        for i in range(Z):
-            agx(h, i).wait_recv()
+        for j in range(Z):
+            for u in range(SUB):
+                agx(h, j, u).wait_recv()
 
     def prune(k):
         wcopy(k).wait()
+        if k + AHEAD < 12:
+            wcopy(k + AHEAD).start()
         which, part = k // 4, k % 4
         w = (gw, uw, dw)[which]
         m = (gm, um, dm)[which]
@@ -249,21 +268,20 @@
 
     ag_start(0)
     order = list(range(12))
-    per = 2
-    for i in range(1, Z):
-        for k in order[:per]:
+    for s in range(1, Z):
+        for k in order[:1]:
             prune(k)
-        order = order[per:]
-        ag_forward(0, i)
+        order = order[1:]
+        ag_hop(0, s)
     ag_start(1)
     for k in order:
         prune(k)
     ag_finish(0)
     plan = [(q, False) for q in range(groups)] + [(q, True) for q in range(groups)]
     for n, (q, mine) in enumerate(plan):
+        if n + 1 < Z:
+            ag_hop(1, n + 1)
         group(0, q, mine)
-        if n + 1 < Z:
-            ag_forward(1, n + 1)
     hidden(0)
     down(0)
     ag_finish(1)
@@ -284,10 +302,10 @@
     out[:, cols(1 - d)] = finrx[...]
     first.wait_send()
     for h in range(2):
-        for i in range(Z):
-            agx(h, i).wait_send()
-        for i in range(1, Z):
-            agz(h, i).wait_send()
+        for j in range(Z):
+            for u in range(SUB):
+                agx(h, j, u).wait_send()
+                relay(h, j, u, lambda c: c.wait_send())
 
 
 def fused(Z, tokens, ln_gain, gate_weight, up_weight, down_weight, gate_mask, up_mask, down_mask):
@@ -327,8 +345,8 @@
             pltpu.VMEM((ROWS, kl), BF16),
             dma((12,)),
             dma, dma,
-            dma((2, Z - 1)), dma((2, Z - 1)),
-            dma((2, Z)), dma((2, Z)),
+            dma((2, 2, Z * SUB)), dma((2, Z * SUB)),
+            dma((2, Z * SUB)), dma((2, Z * SUB)),
             dma((2, groups)), dma((2, groups)),
             dma((2, groups)), dma((2, groups)),
             dma((2, chunks)), dma((2, chunks)),

time: 83.2 us -> 85.4 us (1.026)
  Pallas kernels: 79.8 us -> 82 us
    pallas_call x1, Pallas kernels: 79.8 us -> 82 us  [fused(): pl.pallas_call(functools.partial(fused_kernel, Z), out_shape=jax.ShapeDty...]
where the time goes in v1:
time: 85.4 us; the launch traced here: 85.1 us
  Pallas kernels  82 us (96%)
  local copies, waits for them, and re-layouts  3.16 us (4%)
    pallas_call x1, Pallas kernels, fused(): pl.pallas_call(functools.partial(fused_kernel, Z), out_shape=jax.ShapeDty...  82 us
    unnamed x2, local copies, waits for them, and re-layouts  3.16 us

profile of v1, /device:TPU:0, one launch (start us, length us, event | category | flops | bytes accessed | tf_op | source)
XLA Modules:
  0.0 85.1 jit_solution(9307313253005396060)
XLA Ops:
  0.0 1.5 %copy.9.dm = s32[128,64]{1,0:T(8,128)} copy(s32[128,64]{0,1:T(8,128)} %param.15) | data formatting | bytes 65536 | tf_op args[7]
  1.5 82.0 %shard_map.82 = bf16[16,8192]{1,0:T(8,128)(2,1)} custom-call(s32[64,128]{1,0:T(8,128)} %gm.1, s32[64,128]{1,0:T(8,128)} %um.1, s32[128,64]{1,0:T(8,128)} %copy.9.dm, bf16[16,8192]{1,0:T(8,128)(2,1)} %tok.1, f32[1,8192]{1,0:T(1,128)} %bitcast.1, bf16[4096,2048]{1,0:T(8,128)(2,1)} %gw_hbm.1, bf16[4096,2048]{1,0:T(8,128)(2,1)} %uw_hbm.1, bf16[2048,4096]{1,0:T(8,128)(2,1)} %dw_hbm.1), custom_call_target="tpu_custom_call" | custom-call | flops 12884901888 | bytes 50331648 | tf_op jit(solution)/shard_map/pallas_call | solution.py:324
  83.5 1.7 %copy.11 = bf16[16,8192]{1,0:T(8,128)(2,1)} copy(bf16[16,8192]{1,0:T(8,128)(2,1)} %shard_map.82) | data formatting | bytes 524288
